TPU v7x, 32 devices: a whole 2x2x4 slice. The times are simulated.
32 devices in a mesh: dp: 8 (over z, y), seq: 4 (over x, core).
Axes of the slice: x: 2, y: 2, z: 4, core: 2. Of those that a mesh axis runs over, the one named last changes fastest.
Arguments:
- hidden_in: bfloat16 [32, 1024, 768], P('dp', 'seq'), may hold values from -6 to 6
- time_table: bfloat16 [1024, 128], replicated, may hold values from -6 to 6
- time_step: int32 [32], P('dp'), may hold values from 0 to 1023
- token_pos: int32 [32, 1024], P('dp', 'seq'), may hold values from 0 to 3071, as said below
- heads_weight: bfloat16 [768, 2304], P('seq'), may hold values from -0.15625 to 0.15625
- merge_weight: bfloat16 [768, 768], P('seq'), may hold values from -1.75 to 1.75
- lift_weight: bfloat16 [768, 3072], P('seq'), may hold values from -0.21875 to 0.21875
- lift_bias: bfloat16 [3072], P('seq'), may hold values from -3 to 3
- drop_weight: bfloat16 [3072, 768], P('seq'), may hold values from -0.109375 to 0.109375
- drop_bias: bfloat16 [768], P('seq'), may hold values from -3 to 3
- modulate_weight: bfloat16 [4608, 128], P('seq'), may hold values from -0.5 to 0.5
- modulate_bias: bfloat16 [4608], P('seq'), may hold values from -3 to 3
- first_gain: bfloat16 [768], P('seq'), may hold values from 0.099609375 to 1.8984375
- second_gain: bfloat16 [768], P('seq'), may hold values from 0.099609375 to 1.8984375
- out_grad: bfloat16 [32, 1024, 768], P('dp', 'seq'), may hold values from -6 to 6
Outputs:
- block_out: bfloat16 [32, 1024, 768], P('dp', 'seq')
- input_grad: bfloat16 [32, 1024, 768], P('dp', 'seq')
- heads_grad: float32 [768, 2304], P('seq')
- merge_grad: float32 [768, 768], P('seq')
- lift_grad: float32 [768, 3072], P('seq')
- liftbias_grad: float32 [3072], P('seq')
- drop_grad: float32 [3072, 768], P('seq')
- dropbias_grad: float32 [768], P('seq')
- modulate_grad: float32 [4608, 128], P('seq')
- modulatebias_grad: float32 [4608], P('seq')
- firstgain_grad: float32 [768], P('seq')
- secondgain_grad: float32 [768], P('seq')
- table_grad: float32 [1024, 128], P('seq')
Inputs may be any that keep to these rules, and one draw needn't show every extreme that they name: `token_pos`: positions count up by one along a row and start again at 0 at each separator token; in every aligned group of 4 rows one row holds no separator; such a row in the first group starts at 2048, such a row in the second group starts at 0.
All inputs are finite; a program needn't handle non-finite values.
Results may differ from a plain program's by a relative error of at most 0.017.
The roundings to bfloat16 on the way count: a program that leaves them out, or rounds other values in their place, can miss the bound.
Values may be sent and summed in bfloat16 or wider, within the bound.
No kernel may reach another device: no remote copies, remote signals or barrier semaphores. Data moves between devices by JAX's collectives and lax.ppermute only.
A program may use at most 320 MiB of HBM per device.

v0:
```python
from functools import partial
import math
import jax
import jax.numpy as jnp
from jax import lax
from jax.sharding import PartitionSpec as P

HEADS = 12
EPSILON = 1e-05


def rotate_half(values):
    middle = values.shape[-1] // 2
    return jnp.concatenate([-values[..., middle:], values[..., :middle]], axis=-1)


def rotate(values, cosine, sine):
    return values * cosine + rotate_half(values) * sine


def unrotate(values, cosine, sine):
    return values * cosine - rotate_half(values * sine)


def norm_forward(values, gain):
    center = values - jnp.mean(values, axis=-1, keepdims=True)
    inverse = lax.rsqrt(jnp.mean(center * center, axis=-1, keepdims=True) + EPSILON)
    unit = center * inverse
    return (unit, inverse, unit * gain)


def norm_backward(normed_grad, unit, inverse, gain):
    unit_grad = normed_grad * gain
    first = jnp.mean(unit_grad, axis=-1, keepdims=True)
    second = jnp.mean(unit_grad * unit, axis=-1, keepdims=True)
    return inverse * (unit_grad - first - unit * second)


def grouping(seqs, span):
    group = 1
    while group * span < 512 and seqs % (group * 2) == 0:
        group = group * 2
    return group


def shards(
    hidden_in,
    time_table,
    time_step,
    token_pos,
    heads_weight,
    merge_weight,
    lift_weight,
    lift_bias,
    drop_weight,
    drop_bias,
    modulate_weight,
    modulate_bias,
    first_gain,
    second_gain,
    out_grad,
):
    float_type = jnp.float32
    low_type = jnp.bfloat16
    position_count = lax.axis_size("seq")
    hidden_rows, upstream_rows, places_rows = (hidden_in, out_grad, token_pos)
    seqs, span, width = hidden_rows.shape
    length = span * position_count
    head_width = width // HEADS
    scale = 1.0 / math.sqrt(head_width)
    gathered = (
        lax.all_gather(heads_weight, "seq", axis=0, tiled=True),
        lax.all_gather(merge_weight, "seq", axis=0, tiled=True),
        lax.all_gather(lift_weight, "seq", axis=0, tiled=True),
        lax.all_gather(lift_bias, "seq", axis=0, tiled=True),
        lax.all_gather(drop_weight, "seq", axis=0, tiled=True),
        lax.all_gather(drop_bias, "seq", axis=0, tiled=True),
        lax.all_gather(modulate_weight, "seq", axis=0, tiled=True),
        lax.all_gather(modulate_bias, "seq", axis=0, tiled=True),
        lax.all_gather(first_gain, "seq", axis=0, tiled=True),
        lax.all_gather(second_gain, "seq", axis=0, tiled=True),
    )
    w_heads, w_merge, w_lift, b_lift, w_drop, b_drop, w_mod, b_mod, gain_one, gain_two = gathered
    gain_one = gain_one.astype(float_type)
    gain_two = gain_two.astype(float_type)
    table_rows = time_table.shape[0]
    choose = (time_step[:, None] == jnp.arange(table_rows, dtype=jnp.int32)[None, :]).astype(
        low_type
    )
    conds = jnp.dot(choose, time_table, preferred_element_type=float_type)
    modulation = lax.dot_general(
        conds.astype(low_type), w_mod, (((1,), (1,)), ((), ())), preferred_element_type=float_type
    ) + b_mod.astype(float_type)
    pieces = [piece[:, None, :] for piece in jnp.split(modulation, 6, axis=-1)]
    shift_a, scale_a, gate_a, shift_b, scale_b, gate_b = pieces
    positions = places_rows.astype(float_type)
    freqs = 10000.0 ** (-jnp.arange(0, head_width, 2, dtype=float_type) / head_width)
    angles = positions[..., None] * freqs
    angles = jnp.concatenate([angles, angles], axis=-1)
    cosine = jnp.cos(angles)[:, :, None, :]
    sine = jnp.sin(angles)[:, :, None, :]
    head_layout = (seqs, span, HEADS, head_width)
    inputs = hidden_rows.astype(float_type)
    unit_one, inverse_one, normed_one = norm_forward(inputs, gain_one)
    adapted_one = (normed_one * (1.0 + scale_a) + shift_a).astype(low_type)
    projected = jnp.einsum("scd,de->sce", adapted_one, w_heads, preferred_element_type=float_type)
    query_raw, key_raw, value_raw = jnp.split(projected, 3, axis=-1)
    query = rotate(query_raw.reshape(head_layout), cosine, sine).astype(low_type)
    keys_local = (
        rotate(key_raw.reshape(head_layout), cosine, sine)
        .astype(low_type)
        .reshape(seqs, span, width)
    )
    values_local = value_raw.astype(low_type)
    keys_all, values_all = (
        lax.all_gather(keys_local, "seq", axis=1, tiled=True),
        lax.all_gather(values_local, "seq", axis=1, tiled=True),
    )
    group = grouping(seqs, span)
    blocks = seqs // group

    def split_groups(array):
        return array.reshape((blocks, group) + array.shape[1:])

    def attend(block):
        query_b, keys_b, values_b = block
        keys_h = keys_b.reshape(group, length, HEADS, head_width)
        values_h = values_b.reshape(group, length, HEADS, head_width)
        scores = (
            jnp.einsum("gqhd,gkhd->ghqk", query_b, keys_h, preferred_element_type=float_type)
            * scale
        )
        peak = jnp.max(scores, axis=-1, keepdims=True)
        expos = jnp.exp(scores - peak)
        totals = jnp.sum(expos, axis=-1, keepdims=True)
        probs = (expos / totals).astype(low_type)
        mixed_b = jnp.einsum("ghqk,gkhd->gqhd", probs, values_h, preferred_element_type=float_type)
        return (mixed_b, peak[..., 0] + jnp.log(totals[..., 0]))

    mixed, logsum = lax.map(
        attend, (split_groups(query), split_groups(keys_all), split_groups(values_all))
    )
    mixed_low = mixed.reshape(seqs, span, width).astype(low_type)
    branch = jnp.einsum("scd,de->sce", mixed_low, w_merge, preferred_element_type=float_type)
    middle = inputs + gate_a * branch
    unit_two, inverse_two, normed_two = norm_forward(middle, gain_two)
    adapted_two = (normed_two * (1.0 + scale_b) + shift_b).astype(low_type)
    upper = jnp.einsum(
        "scd,df->scf", adapted_two, w_lift, preferred_element_type=float_type
    ) + b_lift.astype(float_type)
    active, gelu_back = jax.vjp(partial(jax.nn.gelu, approximate=True), upper)
    active_low = active.astype(low_type)
    lowered = jnp.einsum(
        "scf,fd->scd", active_low, w_drop, preferred_element_type=float_type
    ) + b_drop.astype(float_type)
    block_out = (middle + gate_b * lowered).astype(low_type)
    upstream = upstream_rows.astype(float_type)
    gate_b_grad = jnp.sum(upstream * lowered, axis=1)
    lowered_grad = (gate_b * upstream).astype(low_type)
    drop_grad = jnp.einsum(
        "scf,scd->fd", active_low, lowered_grad, preferred_element_type=float_type
    )
    dropbias_grad = jnp.sum(lowered_grad.astype(float_type), axis=(0, 1))
    active_grad = jnp.einsum("scd,fd->scf", lowered_grad, w_drop, preferred_element_type=float_type)
    (upper_grad,) = gelu_back(active_grad)
    upper_low = upper_grad.astype(low_type)
    lift_grad = jnp.einsum("scd,scf->df", adapted_two, upper_low, preferred_element_type=float_type)
    liftbias_grad = jnp.sum(upper_low.astype(float_type), axis=(0, 1))
    adapted_two_grad = jnp.einsum(
        "scf,df->scd", upper_low, w_lift, preferred_element_type=float_type
    )
    shift_b_grad = jnp.sum(adapted_two_grad, axis=1)
    scale_b_grad = jnp.sum(adapted_two_grad * normed_two, axis=1)
    normed_two_grad = adapted_two_grad * (1.0 + scale_b)
    secondgain_grad = jnp.sum(normed_two_grad * unit_two, axis=(0, 1))
    middle_grad = upstream + norm_backward(normed_two_grad, unit_two, inverse_two, gain_two)
    gate_a_grad = jnp.sum(middle_grad * branch, axis=1)
    branch_grad = (gate_a * middle_grad).astype(low_type)
    merge_grad = jnp.einsum(
        "scd,sce->de", mixed_low, branch_grad, preferred_element_type=float_type
    )
    mixed_grad = jnp.einsum(
        "sce,de->scd", branch_grad, w_merge, preferred_element_type=float_type
    ).astype(low_type)
    keys_back, values_back = (
        lax.all_gather(keys_local, "seq", axis=1, tiled=True),
        lax.all_gather(values_local, "seq", axis=1, tiled=True),
    )

    def attend_back(block):
        query_b, keys_b, values_b, logsum_b, mixed_grad_b = block
        keys_h = keys_b.reshape(group, length, HEADS, head_width)
        values_h = values_b.reshape(group, length, HEADS, head_width)
        scores = (
            jnp.einsum("gqhd,gkhd->ghqk", query_b, keys_h, preferred_element_type=float_type)
            * scale
        )
        probs = jnp.exp(scores - logsum_b[..., None])
        probs_low = probs.astype(low_type)
        values_term = jnp.einsum(
            "ghqk,gqhd->gkhd", probs_low, mixed_grad_b, preferred_element_type=float_type
        )
        probs_grad = jnp.einsum(
            "gqhd,gkhd->ghqk", mixed_grad_b, values_h, preferred_element_type=float_type
        )
        center = jnp.sum(probs * probs_grad, axis=-1, keepdims=True)
        scores_grad = (probs * (probs_grad - center)).astype(low_type)
        query_term = (
            jnp.einsum("ghqk,gkhd->gqhd", scores_grad, keys_h, preferred_element_type=float_type)
            * scale
        )
        keys_term = (
            jnp.einsum("ghqk,gqhd->gkhd", scores_grad, query_b, preferred_element_type=float_type)
            * scale
        )
        return (
            query_term,
            keys_term.reshape(group, length, width),
            values_term.reshape(group, length, width),
        )

    mixed_grad_h = mixed_grad.reshape(head_layout)
    query_term, keys_term, values_term = lax.map(
        attend_back,
        (
            split_groups(query),
            split_groups(keys_back),
            split_groups(values_back),
            logsum,
            split_groups(mixed_grad_h),
        ),
    )
    keys_grad, values_grad = (
        lax.psum_scatter(
            keys_term.reshape(seqs, length, width).astype(jnp.bfloat16),
            "seq",
            scatter_dimension=1,
            tiled=True,
        ).astype(jnp.float32),
        lax.psum_scatter(
            values_term.reshape(seqs, length, width).astype(jnp.bfloat16),
            "seq",
            scatter_dimension=1,
            tiled=True,
        ).astype(jnp.float32),
    )
    query_grad = unrotate(query_term.reshape(head_layout), cosine, sine).reshape(seqs, span, width)
    key_grad = unrotate(keys_grad.reshape(head_layout), cosine, sine).reshape(seqs, span, width)
    projected_grad = jnp.concatenate([query_grad, key_grad, values_grad], axis=-1).astype(low_type)
    heads_grad = jnp.einsum(
        "scd,sce->de", adapted_one, projected_grad, preferred_element_type=float_type
    )
    adapted_one_grad = jnp.einsum(
        "sce,de->scd", projected_grad, w_heads, preferred_element_type=float_type
    )
    shift_a_grad = jnp.sum(adapted_one_grad, axis=1)
    scale_a_grad = jnp.sum(adapted_one_grad * normed_one, axis=1)
    normed_one_grad = adapted_one_grad * (1.0 + scale_a)
    firstgain_grad = jnp.sum(normed_one_grad * unit_one, axis=(0, 1))
    input_grad = (
        middle_grad + norm_backward(normed_one_grad, unit_one, inverse_one, gain_one)
    ).astype(low_type)
    modulation_grad = jnp.concatenate(
        [shift_a_grad, scale_a_grad, gate_a_grad, shift_b_grad, scale_b_grad, gate_b_grad], axis=-1
    )
    modulate_grad = jnp.einsum("sm,sc->mc", modulation_grad, conds, precision=lax.Precision.HIGHEST)
    modulatebias_grad = jnp.sum(modulation_grad, axis=0)
    conds_grad = jnp.einsum(
        "sm,mc->sc", modulation_grad, w_mod.astype(float_type), precision=lax.Precision.HIGHEST
    )
    table_grad = jnp.einsum(
        "sn,sc->nc", choose.astype(float_type), conds_grad, precision=lax.Precision.HIGHEST
    )
    terms = (
        heads_grad,
        merge_grad,
        lift_grad,
        liftbias_grad,
        drop_grad,
        dropbias_grad,
        modulate_grad,
        modulatebias_grad,
        firstgain_grad,
        secondgain_grad,
        table_grad,
    )
    shares = (
        lax.psum_scatter(
            terms[0].astype(jnp.bfloat16), "seq", scatter_dimension=0, tiled=True
        ).astype(jnp.float32),
        lax.psum_scatter(
            terms[1].astype(jnp.bfloat16), "seq", scatter_dimension=0, tiled=True
        ).astype(jnp.float32),
        lax.psum_scatter(
            terms[2].astype(jnp.bfloat16), "seq", scatter_dimension=0, tiled=True
        ).astype(jnp.float32),
        lax.psum_scatter(
            terms[3].astype(jnp.bfloat16), "seq", scatter_dimension=0, tiled=True
        ).astype(jnp.float32),
        lax.psum_scatter(
            terms[4].astype(jnp.bfloat16), "seq", scatter_dimension=0, tiled=True
        ).astype(jnp.float32),
        lax.psum_scatter(
            terms[5].astype(jnp.bfloat16), "seq", scatter_dimension=0, tiled=True
        ).astype(jnp.float32),
        lax.psum_scatter(
            terms[6].astype(jnp.bfloat16), "seq", scatter_dimension=0, tiled=True
        ).astype(jnp.float32),
        lax.psum_scatter(
            terms[7].astype(jnp.bfloat16), "seq", scatter_dimension=0, tiled=True
        ).astype(jnp.float32),
        lax.psum_scatter(
            terms[8].astype(jnp.bfloat16), "seq", scatter_dimension=0, tiled=True
        ).astype(jnp.float32),
        lax.psum_scatter(
            terms[9].astype(jnp.bfloat16), "seq", scatter_dimension=0, tiled=True
        ).astype(jnp.float32),
        lax.psum_scatter(
            terms[10].astype(jnp.bfloat16), "seq", scatter_dimension=0, tiled=True
        ).astype(jnp.float32),
    )
    summed = lax.psum(
        (
            shares[0],
            shares[1],
            shares[2],
            shares[3],
            shares[4],
            shares[5],
            shares[6],
            shares[7],
            shares[8],
            shares[9],
            shares[10],
        ),
        "dp",
    )
    return (
        block_out,
        input_grad,
        summed[0],
        summed[1],
        summed[2],
        summed[3],
        summed[4],
        summed[5],
        summed[6],
        summed[7],
        summed[8],
        summed[9],
        summed[10],
    )


def solution(mesh):
    return jax.shard_map(
        shards,
        mesh=mesh,
        in_specs=(
            P("dp", "seq", None),
            P(),
            P("dp"),
            P("dp", "seq"),
            P("seq", None),
            P("seq", None),
            P("seq", None),
            P("seq"),
            P("seq", None),
            P("seq"),
            P("seq", None),
            P("seq"),
            P("seq"),
            P("seq"),
            P("dp", "seq", None),
        ),
        out_specs=(
            P("dp", "seq", None),
            P("dp", "seq", None),
            P("seq", None),
            P("seq", None),
            P("seq", None),
            P("seq"),
            P("seq", None),
            P("seq"),
            P("seq", None),
            P("seq"),
            P("seq"),
            P("seq"),
            P("seq", None),
        ),
        check_vma=False,
    )
```

profile of v0, /device:TPU:0, one launch (start us, length us, event | category | flops | bytes accessed | tf_op | source)
XLA Modules:
  0.0 1162.3 jit_solution(14610913163980127939)
XLA Ops:
  13.3 8.5 all-reduce.10
  33.2 29.1 %all-gather.12.cloned.1.call-done = bf16[768,2304]{1,0:T(8,128)(2,1)} async-done(((bf16[192,2304]{1,0:T(8,128)(2,1)}), bf16[768,2304]{1,0:T(8,128)(2,1)}) %all-gather.12.cloned.1.call-update) | async-done | bytes 3538960 | tf_op jit(solution)/shard_map/all_gather | solution.py:72
  62.3 6.2 fusion.52
  96.0 6.6 add_convert_fusion.2
  107.2 5.6 all-gather.1
  121.9 8.7 copy.93
  130.6 37.9 %all-gather.16.cloned.1.call-done = bf16[4,1024,768]{2,1,0:T(8,128)(2,1)} async-done(((bf16[4,256,768]{2,1,0:T(8,128)(2,1)}), bf16[4,1024,768]{2,1,0:T(8,128)(2,1)}) %all-gather.16.cloned.1.call-update) | async-done | bytes 6291472 | tf_op jit(solution)/shard_map/all_gather | solution.py:116
  168.5 8.7 copy.94
  177.2 74.9 %while.28 = (s32[]{:T(128)}, bf16[2,2,256,12,64]{2,4,3,1,0:T(8,128)(2,1)}, f32[2,2,12,256]{3,2,1,0:T(8,128)S(1)}, bf16[2,2,1024,768]{2,3,1,0:T(8,128)(2,1)}, bf1...) while((s32[]{:T(128)}, bf16[2,2,256,12,64]{2,4,3,1,0:T(8,128)(2,1)}, ...), condition=%wide.region_5.6_spmd.clone, body=%wide.region_2.5_spmd.sunk.clone | while | flops 1667229696 | bytes 96952408 | solution.py:140
  180.9 10.2 multiply_reduce_fusion.11
  191.1 11.7 %fusion.143 = f32[2,12,256]{2,1,0:T(8,128)S(1)} fusion(f32[2,12,256,1024]{3,2,1,0:T(8,128)} %get-tuple-element.385, f32[2,12,256]{2,1,0:T(8,128)S(1)} %get-tuple-element.386), kind=kLoop, calls=%fused_computation.3.clone.1.clone | loop fusion | flops 18868224 | bytes 25214976 | tf_op jit(solution)/shard_map/while/body/eval_jaxpr/reduce_sum | solution.py:135
  202.8 11.8 %bitcast_dynamic-update-slice_fusion.9 = bf16[2,2,256,12,64]{2,4,3,1,0:T(8,128)(2,1)} fusion(bf16[2,2,256,12,64]{2,4,3,1,0:T(8,128)(2,1)} %get-tuple-element.425, s32[]{:T(128)S(6)} %copy.125, bf16[2,1024,12,64]{1,3,2,0:T(8,128)(2,1)S(1)} %bitcast.191, f32[2,12,256,1024]{3,2,1,0:T(8,128)} %get-tuple-element.385, ...), kind=kOutput, calls=%fused_computation.5.clone.1.clone | convolution fusion | flops 830472192 | bytes 29933572 | tf_op jit(solution)/shard_map/while/body/eval_jaxpr/ghqk,gkhd->gqhd/dot_general | solution.py:137
  218.3 10.3 multiply_reduce_fusion.11
  228.5 11.8 %fusion.143 = f32[2,12,256]{2,1,0:T(8,128)S(1)} fusion(f32[2,12,256,1024]{3,2,1,0:T(8,128)} %get-tuple-element.385, f32[2,12,256]{2,1,0:T(8,128)S(1)} %get-tuple-element.386), kind=kLoop, calls=%fused_computation.3.clone.1.clone | loop fusion | flops 18868224 | bytes 25214976 | tf_op jit(solution)/shard_map/while/body/eval_jaxpr/reduce_sum | solution.py:135
  240.4 11.8 %bitcast_dynamic-update-slice_fusion.9 = bf16[2,2,256,12,64]{2,4,3,1,0:T(8,128)(2,1)} fusion(bf16[2,2,256,12,64]{2,4,3,1,0:T(8,128)(2,1)} %get-tuple-element.425, s32[]{:T(128)S(6)} %copy.125, bf16[2,1024,12,64]{1,3,2,0:T(8,128)(2,1)S(1)} %bitcast.191, f32[2,12,256,1024]{3,2,1,0:T(8,128)} %get-tuple-element.385, ...), kind=kOutput, calls=%fused_computation.5.clone.1.clone | convolution fusion | flops 830472192 | bytes 29933572 | tf_op jit(solution)/shard_map/while/body/eval_jaxpr/ghqk,gkhd->gqhd/dot_general | solution.py:137
  259.5 11.3 fusion.40
  270.8 16.6 %fusion.93 = (bf16[3072]{0:T(1024)(128)(2,1)}, bf16[4,256,3072]{2,1,0:T(8,128)(2,1)}) fusion(f32[4,256,3072]{2,1,0:T(8,128)} %fusion.40, f32[3072]{0:T(1024)S(1)} %bitcast.210, bf16[3072,768]{1,0:T(8,128)(2,1)} %all-gather.22.cloned.1.call-done, bf16[4,256,768]{2,1,0:T(8,128)(2,1)S(1)} %copy-done.27, f32[4,768]{1,0:T(4,128)S(1)} %copy-done.36), kind=kOutput, calls=%fused_computation.174 | convolution fusion | flops 4903400448 | bytes 25196544 | tf_op jit(solution)/shard_map/scd,fd->scf/dot_general | solution.py:164
  287.4 10.2 multiply_reduce_fusion.2
  297.6 15.1 %fusion.67 = (f32[4,768]{1,0:T(4,128)}, bf16[4,256,768]{2,1,0:T(8,128)(2,1)}, f32[4,768]{1,0:T(4,128)}, f32[4,256,768]{2,1,0:T(8,128)S(1)}) fusion(bf16[4,256,768]{2,1,0:T(8,128)(2,1)S(1)} %copy-done.27, f32[768]{0:T(1024)S(1)} %copy-done.65, f32[4,256,768]{2,1,0:T(8,128)S(1)} %copy-done.18, f32[4,768]{1,0:T(4,128)S(1)} %copy-done.36, ...), kind=kOutput, calls=%fused_computation.96 | convolution fusion | flops 4877445120 | bytes 33114112 | tf_op jit(solution)/shard_map/scf,fd->scd/dot_general | solution.py:153
  317.4 178.6 %while.29 = (s32[]{:T(128)}, f32[2,2,256,12,64]{2,4,3,1,0:T(8,128)}, bf16[2,2,1024,768]{2,3,1,0:T(8,128)(2,1)}, bf16[2,2,1024,768]{2,3,1,0:T(8,128)(2,1)}, bf16[...) while((s32[]{:T(128)}, ...), condition=%wide.region_12.13_spmd.clone, body=%wide.region_10.12_spmd.sunk.clone | while | flops 4105562112 | bytes 316326176 | solution.py:223
  323.3 11.5 fusion.153
  334.8 12.2 %fusion.154 = bf16[2,12,64,1024]{3,2,1,0:T(8,128)(2,1)} fusion(f32[2,12,256,1024]{3,2,1,0:T(8,128)} %fusion.153, f32[2,12,256]{2,1,0:T(8,128)S(1)} %dynamic-slice_bitcast_fusion.3, bf16[2,2,256,12,64]{2,4,3,1,0:T(8,128)(2,1)S(1)} %copy-done.6, s32[]{:T(128)S(6)} %copy.135), kind=kOutput, calls=%fused_computation.18.clone.1.clone | convolution fusion | flops 824180736 | bytes 29130756 | tf_op jit(solution)/shard_map/while/body/eval_jaxpr/ghqk,gqhd->gkhd/dot_general | solution.py:200
  347.0 17.6 %multiply_reduce_fusion.12 = (f32[2,12,256]{2,1,0:T(8,128)S(1)}, f32[2,12,256,1024]{3,2,1,0:T(8,128)}) fusion(f32[2,12,256,1024]{3,2,1,0:T(8,128)} %fusion.153, f32[2,12,256]{2,1,0:T(8,128)S(1)} %dynamic-slice_bitcast_fusion.3, bf16[2,1024,12,64]{1,3,2,0:T(8,128)(2,1)} %bitcast.188, bf16[2,2,256,12,64]{2,4,3,1,0:T(8,128)(2,1)} %get-tuple-element.461, ...), kind=kOutput, calls=%fused_computation.15.clone.1.clone | convolution fusion | flops 830466048 | bytes 54312964 | tf_op jit(solution)/shard_map/while/body/eval_jaxpr/gqhd,gkhd->ghqk/dot_general | solution.py:203
  364.6 21.7 %multiply_convert_fusion.9 = bf16[2,12,256,1024]{3,2,1,0:T(8,128)(2,1)} fusion(f32[2,12,256,1024]{3,2,1,0:T(8,128)} %get-tuple-element.404, f32[2,12,256,1024]{3,2,1,0:T(8,128)} %fusion.153, f32[2,12,256]{2,1,0:T(8,128)S(1)} %get-tuple-element.405, f32[2,12,256]{2,1,0:T(8,128)S(1)} %dynamic-slice_bitcast_fusion.3), kind=kLoop, calls=%fused_computation.14.clone.1.clone | loop fusion | flops 31457280 | bytes 62963712 | tf_op jit(solution)/shard_map/while/body/eval_jaxpr/convert_element_type | solution.py:207
  386.3 8.5 bitcast_dynamic-update-slice_fusion.11
  394.8 8.3 broadcast_multiply_fusion.12
  412.4 11.5 fusion.153
  423.9 12.2 %fusion.154 = bf16[2,12,64,1024]{3,2,1,0:T(8,128)(2,1)} fusion(f32[2,12,256,1024]{3,2,1,0:T(8,128)} %fusion.153, f32[2,12,256]{2,1,0:T(8,128)S(1)} %dynamic-slice_bitcast_fusion.3, bf16[2,2,256,12,64]{2,4,3,1,0:T(8,128)(2,1)S(1)} %copy-done.6, s32[]{:T(128)S(6)} %copy.135), kind=kOutput, calls=%fused_computation.18.clone.1.clone | convolution fusion | flops 824180736 | bytes 29130756 | tf_op jit(solution)/shard_map/while/body/eval_jaxpr/ghqk,gqhd->gkhd/dot_general | solution.py:200
  436.1 17.6 %multiply_reduce_fusion.12 = (f32[2,12,256]{2,1,0:T(8,128)S(1)}, f32[2,12,256,1024]{3,2,1,0:T(8,128)}) fusion(f32[2,12,256,1024]{3,2,1,0:T(8,128)} %fusion.153, f32[2,12,256]{2,1,0:T(8,128)S(1)} %dynamic-slice_bitcast_fusion.3, bf16[2,1024,12,64]{1,3,2,0:T(8,128)(2,1)} %bitcast.188, bf16[2,2,256,12,64]{2,4,3,1,0:T(8,128)(2,1)} %get-tuple-element.461, ...), kind=kOutput, calls=%fused_computation.15.clone.1.clone | convolution fusion | flops 830466048 | bytes 54312964 | tf_op jit(solution)/shard_map/while/body/eval_jaxpr/gqhd,gkhd->ghqk/dot_general | solution.py:203
  453.7 21.7 %multiply_convert_fusion.9 = bf16[2,12,256,1024]{3,2,1,0:T(8,128)(2,1)} fusion(f32[2,12,256,1024]{3,2,1,0:T(8,128)} %get-tuple-element.404, f32[2,12,256,1024]{3,2,1,0:T(8,128)} %fusion.153, f32[2,12,256]{2,1,0:T(8,128)S(1)} %get-tuple-element.405, f32[2,12,256]{2,1,0:T(8,128)S(1)} %dynamic-slice_bitcast_fusion.3), kind=kLoop, calls=%fused_computation.14.clone.1.clone | loop fusion | flops 31457280 | bytes 62963712 | tf_op jit(solution)/shard_map/while/body/eval_jaxpr/convert_element_type | solution.py:207
  475.4 8.5 bitcast_dynamic-update-slice_fusion.11
  483.9 8.3 broadcast_multiply_fusion.12
  496.0 8.7 copy.102
  504.7 8.7 copy.106
  520.0 12.4 %bitcast_convert_fusion = bf16[3072,768]{1,0:T(8,128)(2,1)} fusion(bf16[4,256,768]{2,1,0:T(8,128)(2,1)S(1)} %copy-done.28, f32[4,768]{1,0:T(4,128)S(1)} %copy-done.37, f32[4,256,3072]{2,1,0:T(8,128)} %fusion.40, f32[3072]{0:T(1024)S(1)} %bitcast.212), kind=kOutput, calls=%fused_computation.53 | convolution fusion | flops 4868014080 | bytes 18898944 | tf_op jit(solution)/shard_map/scf,scd->fd/dot_general | solution.py:160
  534.4 10.0 bitcast_convert_fusion.1
  548.7 14.7 %reduce-scatter.9.cloned.1.call-done = bf16[4,256,768]{2,1,0:T(8,128)(2,1)} async-done(((bf16[4,1024,768]{2,1,0:T(8,128)(2,1)}), bf16[4,256,768]{2,1,0:T(8,128)(2,1)}) %reduce-scatter.9.cloned.1.call-update) | async-done | bytes 1572880 | tf_op jit(solution)/shard_map/reduce_scatter | solution.py:234
  582.9 7.0 subtract_convert_fusion.1
  589.9 34.6 %reduce-scatter.11.cloned.1.call-done = bf16[4,256,768]{2,1,0:T(8,128)(2,1)} async-done(((bf16[4,1024,768]{2,1,0:T(8,128)(2,1)}), bf16[4,256,768]{2,1,0:T(8,128)(2,1)}) %reduce-scatter.11.cloned.1.call-update) | async-done | bytes 1572880 | tf_op jit(solution)/shard_map/reduce_scatter | solution.py:240
  624.6 9.1 fusion.64
  641.1 7.9 bitcast_convert_fusion.2
  653.3 50.5 %reduce-scatter.19.cloned.1.call-done = bf16[768,768]{1,0:T(8,128)(2,1)} async-done(((bf16[3072,768]{1,0:T(8,128)(2,1)}), bf16[768,768]{1,0:T(8,128)(2,1)}) %reduce-scatter.19.cloned.1.call-update) | async-done | bytes 1179664 | tf_op jit(solution)/shard_map/reduce_scatter | solution.py:300
  703.8 50.3 %reduce-scatter.17.cloned.1.call-done = bf16[192,3072]{1,0:T(8,128)(2,1)} async-done(((bf16[768,3072]{1,0:T(8,128)(2,1)}), bf16[192,3072]{1,0:T(8,128)(2,1)}) %reduce-scatter.17.cloned.1.call-update) | async-done | bytes 1179664 | tf_op jit(solution)/shard_map/reduce_scatter | solution.py:294
  754.2 10.3 all-reduce.9
  769.3 8.0 reduce-scatter.23.cloned.1.call-done
  777.4 28.7 %reduce-scatter.21.cloned.1.call-done = bf16[1152,128]{1,0:T(8,128)(2,1)} async-done(((bf16[4608,128]{1,0:T(8,128)(2,1)}), bf16[1152,128]{1,0:T(8,128)(2,1)}) %reduce-scatter.21.cloned.1.call-update) | async-done | bytes 294928 | tf_op jit(solution)/shard_map/reduce_scatter | solution.py:306
  806.1 43.0 %reduce-scatter.13.cloned.1.call-done = bf16[192,2304]{1,0:T(8,128)(2,1)} async-done(((bf16[768,2304]{1,0:T(8,128)(2,1)}), bf16[192,2304]{1,0:T(8,128)(2,1)}) %reduce-scatter.13.cloned.1.call-update) | async-done | bytes 884752 | tf_op jit(solution)/shard_map/reduce_scatter | solution.py:288
  849.1 306.4 %all-reduce.12 = (f32[192,2304]{1,0:T(8,128)}, f32[192,768]{1,0:T(8,128)}, f32[192,3072]{1,0:T(8,128)}, f32[768]{0:T(1024)}, f32[768,768]{1,0:T(8,128)}, /*index...) all-reduce(bf16[192,2304]{1,0:T(8,128)(2,1)} %reduce-scatter.13.clo, ...), channel_id=1, replica_groups=mesh['dp'=8,'seq'=4] {'dp'}, use_global_device_ids=true, to_apply=%region_18.19 | all-reduce | flops 1952192 | bytes 11718144 | tf_op jit(solution)/shard_map/psum | solution.py:322
  (292 shorter events, 141.8 us)
Async XLA Ops:
  7.2 22.9 %copy-start = (bf16[1024,128]{1,0:T(8,128)(2,1)S(1)}, bf16[1024,128]{1,0:T(8,128)(2,1)}, u32[]{:S(2)}) copy-start(bf16[1024,128]{1,0:T(8,128)(2,1)} %param.20) | copy-start | bytes 786436
  7.2 22.2 %copy-start.10 = (bf16[4,256,768]{2,1,0:T(8,128)(2,1)S(1)}, bf16[4,256,768]{2,1,0:T(8,128)(2,1)}, u32[]{:S(2)}) copy-start(bf16[4,256,768]{2,1,0:T(8,128)(2,1)} %param.19) | copy-start | bytes 4718596
  7.2 22.9 %copy-start.71 = (s32[4]{0:T(128)S(1)}, s32[4]{0:T(128)}, u32[]{:S(2)}) copy-start(s32[4]{0:T(128)} %param.21) | copy-start | bytes 52
  7.2 23.1 %all-gather.10.cloned.1.call-start = ((), (), s32[]{:S(2)}) async-start(), calls=%async_computation.8 | async-start | bytes 1474560 | tf_op jit(solution)/shard_map/all_gather | solution.py:78
  8.0 54.3 %all-gather.12.cloned.1.call-start = ((), (), s32[]{:S(2)}) async-start(), calls=%async_computation.9 | async-start | bytes 4423680 | tf_op jit(solution)/shard_map/all_gather | solution.py:72
  8.7 113.2 %all-gather.14.cloned.1.call-start = ((), (), s32[]{:S(2)}) async-start(), calls=%async_computation.10 | async-start | bytes 7864320 | tf_op jit(solution)/shard_map/all_gather | solution.py:117
  21.7 46.7 %copy-start.42 = (f32[768]{0:T(1024)}, f32[768]{0:T(1024)S(1)}, u32[]{:S(2)}) copy-start(f32[768]{0:T(1024)S(1)} %convert_element_type.165) | copy-start | bytes 9220
  29.4 39.0 %copy-start.40 = (f32[4,256]{1,0:T(4,128)}, f32[4,256]{1,0:T(4,128)S(1)}, u32[]{:S(2)}) copy-start(f32[4,256]{1,0:T(4,128)S(1)} %broadcast_multiply_fusion.9) | copy-start | bytes 12292
  30.1 38.4 %copy-start.44 = (f32[4,256]{1,0:T(4,128)}, f32[4,256]{1,0:T(4,128)S(1)}, u32[]{:S(2)}) copy-start(f32[4,256]{1,0:T(4,128)S(1)} %add_rsqrt_fusion.1) | copy-start | bytes 12292
  33.2 35.3 %copy-start.34 = (f32[4,768]{1,0:T(4,128)}, f32[4,768]{1,0:T(4,128)S(1)}, u32[]{:S(2)}) copy-start(f32[4,768]{1,0:T(4,128)S(1)} %get-tuple-element.257) | copy-start | bytes 36868
  33.2 35.3 %copy-start.48 = (f32[4,768]{1,0:T(4,128)}, f32[4,768]{1,0:T(4,128)S(1)}, u32[]{:S(2)}) copy-start(f32[4,768]{1,0:T(4,128)S(1)} %get-tuple-element.256) | copy-start | bytes 36868
  73.5 95.0 %all-gather.16.cloned.1.call-start = ((), (), s32[]{:S(2)}) async-start(), calls=%async_computation.11 | async-start | bytes 7864320 | tf_op jit(solution)/shard_map/all_gather | solution.py:116
  74.6 15.8 %copy-start.24 = (f32[4,256,64]{1,2,0:T(8,128)}, f32[4,256,64]{1,2,0:T(8,128)S(1)}, u32[]{:S(2)}) copy-start(f32[4,256,64]{1,2,0:T(8,128)S(1)} %get-tuple-element.250) | copy-start | bytes 786436
  79.2 16.8 %copy-start.8 = (f32[4,256,768]{2,1,0:T(8,128)}, f32[4,256,768]{2,1,0:T(8,128)S(1)}, u32[]{:S(2)}) copy-start(f32[4,256,768]{2,1,0:T(8,128)S(1)} %copy.90) | copy-start | bytes 9437188
  102.7 149.5 %all-gather.18.cloned.1.call-start = ((), (), s32[]{:S(2)}) async-start(), calls=%async_computation.12 | async-start | bytes 1474560 | tf_op jit(solution)/shard_map/all_gather | solution.py:73
  103.3 156.1 %all-gather.20.cloned.1.call-start = ((), (), s32[]{:S(2)}) async-start(), calls=%async_computation.13 | async-start | bytes 5898240 | tf_op jit(solution)/shard_map/all_gather | solution.py:74
  103.8 166.9 %all-gather.22.cloned.1.call-start = ((), (), s32[]{:S(2)}) async-start(), calls=%async_computation.14 | async-start | bytes 5898240 | tf_op jit(solution)/shard_map/all_gather | solution.py:76
  104.6 458.9 %reduce-scatter.9.cloned.1.call-start = ((), (), s32[]{:S(2)}) async-start(), calls=%async_computation.15 | async-start | bytes 7864320 | tf_op jit(solution)/shard_map/reduce_scatter | solution.py:234
  177.2 75.0 %copy-start.11 = (bf16[4,256,768]{2,1,0:T(8,128)(2,1)S(1)}, bf16[4,256,768]{2,1,0:T(8,128)(2,1)}, u32[]{:S(2)}) copy-start(bf16[4,256,768]{2,1,0:T(8,128)(2,1)} %param.19) | copy-start | bytes 4718596
  177.2 75.0 %copy-start.38 = (f32[4,768]{1,0:T(4,128)S(1)}, f32[4,768]{1,0:T(4,128)}, u32[]{:S(2)}) copy-start(f32[4,768]{1,0:T(4,128)} %get-tuple-element.258) | copy-start | bytes 36868
  257.3 40.3 %copy-start.46 = (f32[4,256]{1,0:T(4,128)}, f32[4,256]{1,0:T(4,128)S(1)}, u32[]{:S(2)}) copy-start(f32[4,256]{1,0:T(4,128)S(1)} %broadcast_multiply_fusion.8) | copy-start | bytes 12292
  259.4 38.2 %copy-start.67 = (f32[4,256]{1,0:T(4,128)}, f32[4,256]{1,0:T(4,128)S(1)}, u32[]{:S(2)}) copy-start(f32[4,256]{1,0:T(4,128)S(1)} %add_rsqrt_fusion) | copy-start | bytes 12292
  259.4 11.3 copy-start.27
  270.8 16.6 %copy-start.18 = (f32[4,256,768]{2,1,0:T(8,128)S(1)}, f32[4,256,768]{2,1,0:T(8,128)}, u32[]{:S(2)}) copy-start(f32[4,256,768]{2,1,0:T(8,128)} %copy-done.17) | copy-start | bytes 9437188
  270.8 16.6 %copy-start.73 = (bf16[768,3072]{1,0:T(8,128)(2,1)S(1)}, bf16[768,3072]{1,0:T(8,128)(2,1)}, u32[]{:S(2)}) copy-start(bf16[768,3072]{1,0:T(8,128)(2,1)} %all-gather.20.cloned.1.call-done) | copy-start | bytes 14155780
  297.6 16.7 %copy-start.31 = (bf16[768,768]{1,0:T(8,128)(2,1)S(1)}, bf16[768,768]{1,0:T(8,128)(2,1)}, u32[]{:S(2)}) copy-start(bf16[768,768]{1,0:T(8,128)(2,1)} %all-gather.18.cloned.1.call-done) | copy-start | bytes 3538948
  323.3 11.5 copy-start.6
  364.6 21.7 %copy-start.14 = (f32[2,2,256,12,64]{2,4,3,1,0:T(8,128)S(1)}, f32[2,2,256,12,64]{2,4,3,1,0:T(8,128)}, u32[]{:S(2)}) copy-start(f32[2,2,256,12,64]{2,4,3,1,0:T(8,128)} %get-tuple-element.446) | copy-start | bytes 9437188 | tf_op jit(solution)/shard_map/while
  412.4 11.5 copy-start.6
  453.7 21.7 %copy-start.14 = (f32[2,2,256,12,64]{2,4,3,1,0:T(8,128)S(1)}, f32[2,2,256,12,64]{2,4,3,1,0:T(8,128)}, u32[]{:S(2)}) copy-start(f32[2,2,256,12,64]{2,4,3,1,0:T(8,128)} %get-tuple-element.446) | copy-start | bytes 9437188 | tf_op jit(solution)/shard_map/while
  504.6 119.9 %reduce-scatter.11.cloned.1.call-start = ((), (), s32[]{:S(2)}) async-start(), calls=%async_computation.16 | async-start | bytes 7864320 | tf_op jit(solution)/shard_map/reduce_scatter | solution.py:240
  513.4 139.9 %reduce-scatter.15.cloned.1.call-start = ((), (), s32[]{:S(2)}) async-start(), calls=%async_computation.18 | async-start | bytes 1474560 | tf_op jit(solution)/shard_map/reduce_scatter | solution.py:291
  519.9 183.9 %reduce-scatter.19.cloned.1.call-start = ((), (), s32[]{:S(2)}) async-start(), calls=%async_computation.20 | async-start | bytes 5898240 | tf_op jit(solution)/shard_map/reduce_scatter | solution.py:300
  532.5 221.6 %reduce-scatter.17.cloned.1.call-start = ((), (), s32[]{:S(2)}) async-start(), calls=%async_computation.19 | async-start | bytes 5898240 | tf_op jit(solution)/shard_map/reduce_scatter | solution.py:294
  544.4 233.0 %reduce-scatter.23.cloned.1.call-start = ((), (), s32[]{:S(2)}) async-start(), calls=%async_computation.22 | async-start | bytes 327680 | tf_op jit(solution)/shard_map/reduce_scatter | solution.py:318
  548.7 17.8 %copy-start.25 = (f32[4,256,64]{1,2,0:T(8,128)S(1)}, f32[4,256,64]{1,2,0:T(8,128)}, u32[]{:S(2)}) copy-start(f32[4,256,64]{1,2,0:T(8,128)} %copy-done.24) | copy-start | bytes 786436
  582.9 41.6 %copy-start.35 = (f32[4,768]{1,0:T(4,128)S(1)}, f32[4,768]{1,0:T(4,128)}, u32[]{:S(2)}) copy-start(f32[4,768]{1,0:T(4,128)} %copy-done.34) | copy-start | bytes 36868
  582.9 41.6 %copy-start.41 = (f32[4,256]{1,0:T(4,128)S(1)}, f32[4,256]{1,0:T(4,128)}, u32[]{:S(2)}) copy-start(f32[4,256]{1,0:T(4,128)} %copy-done.40) | copy-start | bytes 12292
  582.9 41.6 %copy-start.43 = (f32[768]{0:T(1024)S(1)}, f32[768]{0:T(1024)}, u32[]{:S(2)}) copy-start(f32[768]{0:T(1024)} %copy-done.42) | copy-start | bytes 9220
  582.9 41.6 %copy-start.45 = (f32[4,256]{1,0:T(4,128)S(1)}, f32[4,256]{1,0:T(4,128)}, u32[]{:S(2)}) copy-start(f32[4,256]{1,0:T(4,128)} %copy-done.44) | copy-start | bytes 12292
  624.6 11.4 copy-start.61
  635.9 170.2 %reduce-scatter.21.cloned.1.call-start = ((), (), s32[]{:S(2)}) async-start(), calls=%async_computation.21 | async-start | bytes 1474560 | tf_op jit(solution)/shard_map/reduce_scatter | solution.py:306
  640.8 208.3 %reduce-scatter.13.cloned.1.call-start = ((), (), s32[]{:S(2)}) async-start(), calls=%async_computation.17 | async-start | bytes 4423680 | tf_op jit(solution)/shard_map/reduce_scatter | solution.py:288
  649.0 105.1 %copy-start.62 = (bf16[3072]{0:T(1024)(128)(2,1)S(1)}, bf16[3072]{0:T(1024)(128)(2,1)}, u32[]{:S(2)}) copy-start(bf16[3072]{0:T(1024)(128)(2,1)} %get-tuple-element.264) | copy-start | bytes 18436
  649.0 105.1 %copy-start.70 = (bf16[768]{0:T(1024)(128)(2,1)S(1)}, bf16[768]{0:T(1024)(128)(2,1)}, u32[]{:S(2)}) copy-start(bf16[768]{0:T(1024)(128)(2,1)} %get-tuple-element.160) | copy-start | bytes 4612
  764.8 84.3 %copy-start.30 = (bf16[768,768]{1,0:T(8,128)(2,1)S(1)}, bf16[768,768]{1,0:T(8,128)(2,1)}, u32[]{:S(2)}) copy-start(bf16[768,768]{1,0:T(8,128)(2,1)} %reduce-scatter.19.cloned.1.call-done) | copy-start | bytes 3538948
  764.8 84.3 %copy-start.33 = (bf16[192,768]{1,0:T(8,128)(2,1)S(1)}, bf16[192,768]{1,0:T(8,128)(2,1)}, u32[]{:S(2)}) copy-start(bf16[192,768]{1,0:T(8,128)(2,1)} %reduce-scatter.15.cloned.1.call-done) | copy-start | bytes 884740
  764.8 390.7 %copy-start.1 = (bf16[1024,128]{1,0:T(8,128)(2,1)S(1)}, bf16[1024,128]{1,0:T(8,128)(2,1)}, u32[]{:S(2)}) copy-start(bf16[1024,128]{1,0:T(8,128)(2,1)} %param.20) | copy-start | bytes 786436
  (48 other events, 245.8 us)
Sparse Core Ops, SparseCore 0:
  9.6 20.2 all-gather.9
  31.5 30.7 all-gather.11
  73.6 46.4 all-gather.13
  122.1 46.3 all-gather.15
  169.9 17.4 all-gather.17
  188.8 37.4 all-gather.19
  227.9 37.4 all-gather.21
  504.8 58.6 reduce-scatter.8
  566.1 58.3 reduce-scatter.10
  627.5 25.7 reduce-scatter.14
  656.0 47.8 reduce-scatter.18
  706.2 47.8 reduce-scatter.16
  757.3 20.0 reduce-scatter.22
  780.3 25.7 reduce-scatter.20
  808.7 40.4 reduce-scatter.12
where the time goes:
time: 1170 us; the launch traced here: 1160 us
  blocking collectives  336 us (29%)
  waiting for transfers between devices  302 us (26%)
  matrix products  279 us (24%)
  local copies, waits for them, and re-layouts  113 us (10%)
  other arithmetic  113 us (10%)
  between operations  17.8 us (2%)
    psum x1, blocking collectives, shards(): lax.psum((shares[0], shares[1], shares[2], shares[3], shares[4], shares[5...  306 us
    reduce_scatter x1, waiting for transfers between devices, shards(): lax.psum_scatter(terms[4].astype(jnp.bfloat16), 'seq', scatter_dimension=...  50.5 us
    reduce_scatter x1, waiting for transfers between devices, shards(): lax.psum_scatter(terms[2].astype(jnp.bfloat16), 'seq', scatter_dimension=...  50.3 us
    convert_element_type x2, other arithmetic, attend_back(): scores_grad = (probs * (probs_grad - center)).astype(low_type)  43.4 us
    reduce_scatter x1, waiting for transfers between devices, shards(): lax.psum_scatter(terms[0].astype(jnp.bfloat16), 'seq', scatter_dimension=...  43 us
    all_gather x1, waiting for transfers between devices, shards(): lax.all_gather(keys_local, 'seq', axis=1, tiled=True)  37.9 us
    dot_general x2, matrix products, attend_back(): jnp.einsum('gqhd,gkhd->ghqk', mixed_grad_b, values_h, preferred_element_t...  35.2 us
    reduce_scatter x1, waiting for transfers between devices, shards(): lax.psum_scatter(values_term.reshape(seqs, length, width).astype(jnp.bflo...  34.6 us
  transfers between devices with their start and end apart: 15, of which 10 were waited for; matrix products, arithmetic and copies ran while one was open for 22% of the time, Pallas kernels for 0%

commit v1 on v0

--- a/solution.py
+++ b/solution.py
@@ -1,3 +1,4 @@
+import functools
 from functools import partial
 import math
 import jax
@@ -7,6 +8,26 @@
 
 HEADS = 12
 EPSILON = 1e-05
+
+
+def push_zone(content, device_axis):
+    parts_n = lax.axis_size(device_axis)
+    inbox = [(k0, (k0 + 1) % parts_n) for k0 in range(parts_n)]
+    trail = [(k0, (k0 - 1) % parts_n) for k0 in range(parts_n)]
+    high, carry = ([content], [content])
+    for _ in range(parts_n // 2):
+        y1 = lax.ppermute(high[-1], device_axis, inbox)
+        high.append(y1)
+    for _ in range((parts_n - 1) // 2):
+        last = lax.ppermute(carry[-1], device_axis, trail)
+        carry.append(last)
+    part_now = jnp.concatenate([*high[::-1], *carry[1:]], axis=1)
+    r1 = lax.axis_index(device_axis)
+    arr_next = jnp.roll(part_now, (r1 - parts_n // 2) * content.shape[1], axis=1)
+    return arr_next
+
+
+number_joints_over_axis = functools.partial(push_zone, device_axis="seq")
 
 
 def rotate_half(values):
@@ -113,7 +134,7 @@
     )
     values_local = value_raw.astype(low_type)
     keys_all, values_all = (
-        lax.all_gather(keys_local, "seq", axis=1, tiled=True),
+        number_joints_over_axis(keys_local),
         lax.all_gather(values_local, "seq", axis=1, tiled=True),
     )
     group = grouping(seqs, span)

time: 1170 us -> 1250 us (1.068)
  local copies, waits for them, and re-layouts: 113 us -> 140 us
  blocking collectives: 336 us -> 356 us
  waiting for transfers between devices: 302 us -> 321 us
    ppermute x0 -> x3, waiting for transfers between devices: none -> 55.5 us  [the longest x2 30.6 us: push_zone(): y1 = lax.ppermute(high[-1], device_axis, inbox)]
    all_gather x1, waiting for transfers between devices: 37.9 us -> 0.01 us  [shards(): lax.all_gather(keys_local, 'seq', axis=1, tiled=True)]
    dynamic_slice x6 -> x12, local copies, waits for them, and re-layouts: 16.7 us -> 39.9 us  [shards(): lax.map(attend, (split_groups(query), split_groups(keys_all), split_group...]
    all_gather x1, blocking collectives: 5.65 us -> 26 us  [shards(): lax.all_gather(lift_bias, 'seq', axis=0, tiled=True)]
  transfers between devices with their start and end apart: 15 -> 18, of which waited for: 10 -> 11; matrix products, arithmetic and copies ran while one was open for 22% -> 26% of each run, Pallas kernels for 0% -> 0%
where the time goes in v1:
time: 1250 us; the launch traced here: 1240 us
  blocking collectives  356 us (28%)
  waiting for transfers between devices  321 us (26%)
  matrix products  288 us (23%)
  local copies, waits for them, and re-layouts  140 us (11%)
  other arithmetic  113 us (9%)
  between operations  18 us (1%)
    psum x1, blocking collectives, shards(): lax.psum((shares[0], shares[1], shares[2], shares[3], shares[4], shares[5...  306 us
    reduce_scatter x1, waiting for transfers between devices, shards(): lax.psum_scatter(terms[4].astype(jnp.bfloat16), 'seq', scatter_dimension=...  50.6 us
    reduce_scatter x1, waiting for transfers between devices, shards(): lax.psum_scatter(terms[2].astype(jnp.bfloat16), 'seq', scatter_dimension=...  50.3 us
    convert_element_type x2, other arithmetic, attend_back(): scores_grad = (probs * (probs_grad - center)).astype(low_type)  43.4 us
    reduce_scatter x1, waiting for transfers between devices, shards(): lax.psum_scatter(terms[0].astype(jnp.bfloat16), 'seq', scatter_dimension=...  43 us
    dynamic_slice x12, local copies, waits for them, and re-layouts, shards(): lax.map(attend, (split_groups(query), split_groups(keys_all), split_group...  39.9 us
    dot_general x2, matrix products, attend_back(): jnp.einsum('gqhd,gkhd->ghqk', mixed_grad_b, values_h, preferred_element_t...  35.1 us
    reduce_scatter x1, waiting for transfers between devices, shards(): lax.psum_scatter(values_term.reshape(seqs, length, width).astype(jnp.bflo...  34.6 us
  transfers between devices with their start and end apart: 18, of which 11 were waited for; matrix products, arithmetic and copies ran while one was open for 26% of the time, Pallas kernels for 0%

profile of v1, /device:TPU:0, one launch (start us, length us, event | category | flops | bytes accessed | tf_op | source)
XLA Modules:
  0.0 1238.9 jit_solution(10977989951317901413)
XLA Ops:
  13.3 8.5 all-reduce.10
  33.2 29.1 %all-gather.12.cloned.1.call-done = bf16[768,2304]{1,0:T(8,128)(2,1)} async-done(((bf16[192,2304]{1,0:T(8,128)(2,1)}), bf16[768,2304]{1,0:T(8,128)(2,1)}) %all-gather.12.cloned.1.call-update) | async-done | bytes 3538960 | tf_op jit(solution)/shard_map/all_gather | solution.py:93
  62.3 6.2 fusion.52
  98.0 6.6 add_convert_fusion.2
  104.7 30.6 %collective-permute-done = bf16[4,256,768]{2,1,0:T(8,128)(2,1)} collective-permute-done((bf16[4,256,768]{2,1,0:T(8,128)(2,1)}, bf16[4,256,768]{2,1,0:T(8,128)(2,1)}, u32[]{:S(2)}, u32[]{:S(2)}) %collective-permute-start) | collective-permute-done | bytes 1572896 | tf_op jit(solution)/shard_map/ppermute | solution.py:19
  136.6 26.0 %all-gather.1 = bf16[4,1,768]{2,1,0:T(2,128)(2,1)S(1)} all-gather(bf16[1,1,768]{2,1,0:T(2,128)(2,1)S(1)} %reshape.233), channel_id=1, replica_groups=mesh['dp'=8,'seq'=4] {'seq'}, dimensions={0}, use_global_device_ids=true | all-gather | bytes 7680 | tf_op jit(solution)/shard_map/all_gather | solution.py:96
  175.3 24.8 %collective-permute-done.2 = bf16[4,256,768]{2,1,0:T(8,128)(2,1)} collective-permute-done((bf16[4,256,768]{2,1,0:T(8,128)(2,1)}, bf16[4,256,768]{2,1,0:T(8,128)(2,1)}, u32[]{:S(2)}, u32[]{:S(2)}) %collective-permute-start.2) | collective-permute-done | bytes 1572896 | tf_op jit(solution)/shard_map/ppermute | solution.py:22
  209.7 8.6 copy.92
  218.3 90.9 %while.28 = (s32[]{:T(128)}, bf16[2,2,256,12,64]{2,4,3,1,0:T(8,128)(2,1)}, f32[2,2,12,256]{3,2,1,0:T(8,128)S(1)}, bf16[2,2,1024,768]{2,3,1,0:T(8,128)(2,1)}, bf1...) while((s32[]{:T(128)}, bf16[2,2,256,12,64]{2,4,3,1,0:T(8,128)(2,1)}, ...), condition=%wide.region_5.6_spmd.clone, body=%wide.region_2.5_spmd.sunk.clone | while | flops 1667229696 | bytes 134717632 | solution.py:161
  229.2 10.2 multiply_reduce_fusion.11
  239.4 13.0 %fusion.143 = f32[2,12,256]{2,1,0:T(8,128)S(1)} fusion(f32[2,12,256,1024]{3,2,1,0:T(8,128)} %get-tuple-element.377, f32[2,12,256]{2,1,0:T(8,128)S(1)} %get-tuple-element.378), kind=kLoop, calls=%fused_computation.3.clone.1.clone | loop fusion | flops 18868224 | bytes 25214976 | tf_op jit(solution)/shard_map/while/body/eval_jaxpr/reduce_sum | solution.py:156
  252.5 10.9 bitcast_dynamic-update-slice_fusion.9
  275.4 10.2 multiply_reduce_fusion.11
  285.6 11.6 fusion.143
  297.2 10.8 bitcast_dynamic-update-slice_fusion.9
  315.5 10.8 fusion.40
  326.3 28.7 %fusion.93 = (bf16[3072]{0:T(1024)(128)(2,1)}, bf16[4,256,3072]{2,1,0:T(8,128)(2,1)}) fusion(f32[4,256,3072]{2,1,0:T(8,128)} %fusion.40, f32[3072]{0:T(1024)S(1)} %bitcast.212, bf16[3072,768]{1,0:T(8,128)(2,1)} %all-gather.20.cloned.1.call-done, bf16[4,256,768]{2,1,0:T(8,128)(2,1)} %param.33, f32[4,768]{1,0:T(4,128)S(1)} %copy-done.37), kind=kOutput, calls=%fused_computation.183 | convolution fusion | flops 4903400448 | bytes 25196544 | tf_op jit(solution)/shard_map/scd,fd->scf/dot_general | solution.py:185
  355.0 10.2 multiply_reduce_fusion.2
  365.3 13.8 %fusion.67 = (f32[4,768]{1,0:T(4,128)}, bf16[4,256,768]{2,1,0:T(8,128)(2,1)}, f32[4,768]{1,0:T(4,128)}, f32[4,256,768]{2,1,0:T(8,128)S(1)}) fusion(bf16[4,256,768]{2,1,0:T(8,128)(2,1)S(1)} %copy-done.28, f32[768]{0:T(1024)S(1)} %copy-done.66, f32[4,256,768]{2,1,0:T(8,128)S(1)} %get-tuple-element.222, f32[4,768]{1,0:T(4,128)S(1)} %copy-done.37, ...), kind=kOutput, calls=%fused_computation.96 | convolution fusion | flops 4877445120 | bytes 33114112 | tf_op jit(solution)/shard_map/scf,fd->scd/dot_general | solution.py:174
  383.8 186.1 %while.29 = (s32[]{:T(128)}, f32[2,2,256,12,64]{2,4,3,1,0:T(8,128)}, bf16[2,2,1024,768]{2,3,1,0:T(8,128)(2,1)}, bf16[2,2,1024,768]{2,3,1,0:T(8,128)(2,1)}, bf16[...) while((s32[]{:T(128)}, ...), condition=%wide.region_12.13_spmd.clone, body=%wide.region_10.12_spmd.sunk.clone | while | flops 4105562112 | bytes 316326144 | solution.py:244
  393.9 11.5 fusion.153
  405.4 12.2 fusion.154
  417.6 17.6 %multiply_reduce_fusion.12 = (f32[2,12,256]{2,1,0:T(8,128)S(1)}, f32[2,12,256,1024]{3,2,1,0:T(8,128)}) fusion(f32[2,12,256,1024]{3,2,1,0:T(8,128)} %fusion.153, f32[2,12,256]{2,1,0:T(8,128)S(1)} %dynamic-slice_bitcast_fusion.3, bf16[2,1024,12,64]{1,3,2,0:T(8,128)(2,1)} %bitcast.189, bf16[2,2,256,12,64]{2,4,3,1,0:T(8,128)(2,1)} %get-tuple-element.453, ...), kind=kOutput, calls=%fused_computation.15.clone.1.clone | convolution fusion | flops 830466048 | bytes 54312964 | tf_op jit(solution)/shard_map/while/body/eval_jaxpr/gqhd,gkhd->ghqk/dot_general | solution.py:224
  435.1 21.7 %multiply_convert_fusion.9 = bf16[2,12,256,1024]{3,2,1,0:T(8,128)(2,1)} fusion(f32[2,12,256,1024]{3,2,1,0:T(8,128)} %get-tuple-element.396, f32[2,12,256,1024]{3,2,1,0:T(8,128)} %fusion.153, f32[2,12,256]{2,1,0:T(8,128)S(1)} %get-tuple-element.397, f32[2,12,256]{2,1,0:T(8,128)S(1)} %dynamic-slice_bitcast_fusion.3), kind=kLoop, calls=%fused_computation.14.clone.1.clone | loop fusion | flops 31457280 | bytes 62963712 | tf_op jit(solution)/shard_map/while/body/eval_jaxpr/convert_element_type | solution.py:228
  456.8 8.6 bitcast_dynamic-update-slice_fusion.11
  465.5 8.1 broadcast_multiply_fusion.12
  486.8 11.5 fusion.153
  498.3 12.2 fusion.154
  510.4 17.6 %multiply_reduce_fusion.12 = (f32[2,12,256]{2,1,0:T(8,128)S(1)}, f32[2,12,256,1024]{3,2,1,0:T(8,128)}) fusion(f32[2,12,256,1024]{3,2,1,0:T(8,128)} %fusion.153, f32[2,12,256]{2,1,0:T(8,128)S(1)} %dynamic-slice_bitcast_fusion.3, bf16[2,1024,12,64]{1,3,2,0:T(8,128)(2,1)} %bitcast.189, bf16[2,2,256,12,64]{2,4,3,1,0:T(8,128)(2,1)} %get-tuple-element.453, ...), kind=kOutput, calls=%fused_computation.15.clone.1.clone | convolution fusion | flops 830466048 | bytes 54312964 | tf_op jit(solution)/shard_map/while/body/eval_jaxpr/gqhd,gkhd->ghqk/dot_general | solution.py:224
  528.0 21.7 %multiply_convert_fusion.9 = bf16[2,12,256,1024]{3,2,1,0:T(8,128)(2,1)} fusion(f32[2,12,256,1024]{3,2,1,0:T(8,128)} %get-tuple-element.396, f32[2,12,256,1024]{3,2,1,0:T(8,128)} %fusion.153, f32[2,12,256]{2,1,0:T(8,128)S(1)} %get-tuple-element.397, f32[2,12,256]{2,1,0:T(8,128)S(1)} %dynamic-slice_bitcast_fusion.3), kind=kLoop, calls=%fused_computation.14.clone.1.clone | loop fusion | flops 31457280 | bytes 62963712 | tf_op jit(solution)/shard_map/while/body/eval_jaxpr/convert_element_type | solution.py:228
  549.7 8.6 bitcast_dynamic-update-slice_fusion.11
  558.4 8.1 broadcast_multiply_fusion.12
  569.9 8.7 copy.101
  578.7 8.7 copy.105
  594.0 12.7 %bitcast_convert_fusion = bf16[3072,768]{1,0:T(8,128)(2,1)} fusion(bf16[4,256,768]{2,1,0:T(8,128)(2,1)S(1)} %copy-done.29, f32[4,768]{1,0:T(4,128)S(1)} %copy-done.38, f32[4,256,3072]{2,1,0:T(8,128)} %fusion.40, f32[3072]{0:T(1024)S(1)} %bitcast.214), kind=kOutput, calls=%fused_computation.53 | convolution fusion | flops 4868014080 | bytes 18898944 | tf_op jit(solution)/shard_map/scf,scd->fd/dot_general | solution.py:181
  608.6 10.0 bitcast_convert_fusion.1
  623.1 16.7 %reduce-scatter.9.cloned.1.call-done = bf16[4,256,768]{2,1,0:T(8,128)(2,1)} async-done(((bf16[4,1024,768]{2,1,0:T(8,128)(2,1)}), bf16[4,256,768]{2,1,0:T(8,128)(2,1)}) %reduce-scatter.9.cloned.1.call-update) | async-done | bytes 1572880 | tf_op jit(solution)/shard_map/reduce_scatter | solution.py:255
  659.3 7.0 subtract_convert_fusion.1
  666.2 34.6 %reduce-scatter.11.cloned.1.call-done = bf16[4,256,768]{2,1,0:T(8,128)(2,1)} async-done(((bf16[4,1024,768]{2,1,0:T(8,128)(2,1)}), bf16[4,256,768]{2,1,0:T(8,128)(2,1)}) %reduce-scatter.11.cloned.1.call-update) | async-done | bytes 1572880 | tf_op jit(solution)/shard_map/reduce_scatter | solution.py:261
  701.0 9.1 fusion.64
  717.5 7.9 bitcast_convert_fusion.2
  729.6 50.6 %reduce-scatter.19.cloned.1.call-done = bf16[768,768]{1,0:T(8,128)(2,1)} async-done(((bf16[3072,768]{1,0:T(8,128)(2,1)}), bf16[768,768]{1,0:T(8,128)(2,1)}) %reduce-scatter.19.cloned.1.call-update) | async-done | bytes 1179664 | tf_op jit(solution)/shard_map/reduce_scatter | solution.py:321
  780.2 50.3 %reduce-scatter.17.cloned.1.call-done = bf16[192,3072]{1,0:T(8,128)(2,1)} async-done(((bf16[768,3072]{1,0:T(8,128)(2,1)}), bf16[192,3072]{1,0:T(8,128)(2,1)}) %reduce-scatter.17.cloned.1.call-update) | async-done | bytes 1179664 | tf_op jit(solution)/shard_map/reduce_scatter | solution.py:315
  830.5 10.3 all-reduce.9
  845.7 8.1 reduce-scatter.23.cloned.1.call-done
  853.7 28.7 %reduce-scatter.21.cloned.1.call-done = bf16[1152,128]{1,0:T(8,128)(2,1)} async-done(((bf16[4608,128]{1,0:T(8,128)(2,1)}), bf16[1152,128]{1,0:T(8,128)(2,1)}) %reduce-scatter.21.cloned.1.call-update) | async-done | bytes 294928 | tf_op jit(solution)/shard_map/reduce_scatter | solution.py:327
  882.5 43.0 %reduce-scatter.13.cloned.1.call-done = bf16[192,2304]{1,0:T(8,128)(2,1)} async-done(((bf16[768,2304]{1,0:T(8,128)(2,1)}), bf16[192,2304]{1,0:T(8,128)(2,1)}) %reduce-scatter.13.cloned.1.call-update) | async-done | bytes 884752 | tf_op jit(solution)/shard_map/reduce_scatter | solution.py:309
  925.5 306.4 %all-reduce.12 = (f32[192,2304]{1,0:T(8,128)}, f32[192,768]{1,0:T(8,128)}, f32[192,3072]{1,0:T(8,128)}, f32[768]{0:T(1024)}, f32[768,768]{1,0:T(8,128)}, /*index...) all-reduce(bf16[192,2304]{1,0:T(8,128)(2,1)} %reduce-scatter.13.clo, ...), channel_id=1, replica_groups=mesh['dp'=8,'seq'=4] {'dp'}, use_global_device_ids=true, to_apply=%region_18.19 | all-reduce | flops 1952192 | bytes 11718144 | tf_op jit(solution)/shard_map/psum | solution.py:343
  (322 shorter events, 177.5 us)
Async XLA Ops:
  7.2 22.9 %copy-start = (bf16[1024,128]{1,0:T(8,128)(2,1)S(1)}, bf16[1024,128]{1,0:T(8,128)(2,1)}, u32[]{:S(2)}) copy-start(bf16[1024,128]{1,0:T(8,128)(2,1)} %param.20) | copy-start | bytes 786436
  7.2 22.3 %copy-start.11 = (bf16[4,256,768]{2,1,0:T(8,128)(2,1)S(1)}, bf16[4,256,768]{2,1,0:T(8,128)(2,1)}, u32[]{:S(2)}) copy-start(bf16[4,256,768]{2,1,0:T(8,128)(2,1)} %param.19) | copy-start | bytes 4718596
  7.2 22.9 %copy-start.72 = (s32[4]{0:T(128)S(1)}, s32[4]{0:T(128)}, u32[]{:S(2)}) copy-start(s32[4]{0:T(128)} %param.21) | copy-start | bytes 52
  7.2 23.1 %all-gather.10.cloned.1.call-start = ((), (), s32[]{:S(2)}) async-start(), calls=%async_computation.8 | async-start | bytes 1474560 | tf_op jit(solution)/shard_map/all_gather | solution.py:99
  8.0 54.3 %all-gather.12.cloned.1.call-start = ((), (), s32[]{:S(2)}) async-start(), calls=%async_computation.9 | async-start | bytes 4423680 | tf_op jit(solution)/shard_map/all_gather | solution.py:93
  8.7 201.0 %all-gather.14.cloned.1.call-start = ((), (), s32[]{:S(2)}) async-start(), calls=%async_computation.10 | async-start | bytes 7864320 | tf_op jit(solution)/shard_map/all_gather | solution.py:138
  21.7 46.7 %copy-start.43 = (f32[768]{0:T(1024)}, f32[768]{0:T(1024)S(1)}, u32[]{:S(2)}) copy-start(f32[768]{0:T(1024)S(1)} %convert_element_type.165) | copy-start | bytes 9220
  29.5 39.0 %copy-start.41 = (f32[4,256]{1,0:T(4,128)}, f32[4,256]{1,0:T(4,128)S(1)}, u32[]{:S(2)}) copy-start(f32[4,256]{1,0:T(4,128)S(1)} %broadcast_multiply_fusion.9) | copy-start | bytes 12292
  30.1 38.4 %copy-start.45 = (f32[4,256]{1,0:T(4,128)}, f32[4,256]{1,0:T(4,128)S(1)}, u32[]{:S(2)}) copy-start(f32[4,256]{1,0:T(4,128)S(1)} %add_rsqrt_fusion.1) | copy-start | bytes 12292
  33.2 35.3 %copy-start.35 = (f32[4,768]{1,0:T(4,128)}, f32[4,768]{1,0:T(4,128)S(1)}, u32[]{:S(2)}) copy-start(f32[4,768]{1,0:T(4,128)S(1)} %get-tuple-element.255) | copy-start | bytes 36868
  33.2 35.3 %copy-start.49 = (f32[4,768]{1,0:T(4,128)}, f32[4,768]{1,0:T(4,128)S(1)}, u32[]{:S(2)}) copy-start(f32[4,768]{1,0:T(4,128)S(1)} %get-tuple-element.254) | copy-start | bytes 36868
  73.5 235.7 %all-gather.16.cloned.1.call-start = ((), (), s32[]{:S(2)}) async-start(), calls=%async_computation.11 | async-start | bytes 1474560 | tf_op jit(solution)/shard_map/all_gather | solution.py:94
  74.1 241.2 %all-gather.18.cloned.1.call-start = ((), (), s32[]{:S(2)}) async-start(), calls=%async_computation.12 | async-start | bytes 5898240 | tf_op jit(solution)/shard_map/all_gather | solution.py:95
  74.7 251.6 %all-gather.20.cloned.1.call-start = ((), (), s32[]{:S(2)}) async-start(), calls=%async_computation.13 | async-start | bytes 5898240 | tf_op jit(solution)/shard_map/all_gather | solution.py:97
  75.2 308.5 %all-gather.22.cloned.1.call-start = ((), (), s32[]{:S(2)}) async-start(), calls=%async_computation.14 | async-start | bytes 7864320 | tf_op jit(solution)/shard_map/all_gather | solution.py:207
  76.4 16.1 %copy-start.25 = (f32[4,256,64]{1,2,0:T(8,128)}, f32[4,256,64]{1,2,0:T(8,128)S(1)}, u32[]{:S(2)}) copy-start(f32[4,256,64]{1,2,0:T(8,128)S(1)} %get-tuple-element.248) | copy-start | bytes 786436
  81.2 16.8 %copy-start.8 = (f32[4,256,768]{2,1,0:T(8,128)}, f32[4,256,768]{2,1,0:T(8,128)S(1)}, u32[]{:S(2)}) copy-start(f32[4,256,768]{2,1,0:T(8,128)S(1)} %copy.89) | copy-start | bytes 9437188
  98.0 37.4 %copy-start.70 = (bf16[768]{0:T(1024)(128)(2,1)S(1)}, bf16[768]{0:T(1024)(128)(2,1)}, u32[]{:S(2)}) copy-start(bf16[768]{0:T(1024)(128)(2,1)} %param.26) | copy-start | bytes 4612
  104.6 30.7 %collective-permute-start = (bf16[4,256,768]{2,1,0:T(8,128)(2,1)}, bf16[4,256,768]{2,1,0:T(8,128)(2,1)}, u32[]{:S(2)}, u32[]{:S(2)}) collective-permute-start(bf16[4,256,768]{2,1,0:T(8,128)(2,1)} %get-tuple-element.229), channel_id=1, source_target_pairs={{0,1},{1,2},{2,3},{3,0},{4,5},{5,6},{6,7},{7,4},{8,9},{9,10},{10,1... | collective-permute-start | bytes 4718600 | tf_op jit(solution)/shard_map/ppermute | solution.py:19
  135.3 36.7 %collective-permute-start.1 = (bf16[4,256,768]{2,1,0:T(8,128)(2,1)}, bf16[4,256,768]{2,1,0:T(8,128)(2,1)}, u32[]{:S(2)}, u32[]{:S(2)}) collective-permute-start(bf16[4,256,768]{2,1,0:T(8,128)(2,1)} %collective-permute-done), channel_id=1, source_target_pairs={{0,1},{1,2},{2,3},{3,0},{4,5},{5,6},{6,7},{7,4},{8,9},{9,10},{10,1... | collective-permute-start | bytes 4718600 | tf_op jit(solution)/shard_map/ppermute | solution.py:19
  163.2 37.0 %collective-permute-start.2 = (bf16[4,256,768]{2,1,0:T(8,128)(2,1)}, bf16[4,256,768]{2,1,0:T(8,128)(2,1)}, u32[]{:S(2)}, u32[]{:S(2)}) collective-permute-start(bf16[4,256,768]{2,1,0:T(8,128)(2,1)} %get-tuple-element.229), channel_id=1, source_target_pairs={{0,3},{1,0},{2,1},{3,2},{4,7},{5,4},{6,5},{7,6},{8,11},{9,8},{10,9... | collective-permute-start | bytes 4718600 | tf_op jit(solution)/shard_map/ppermute | solution.py:22
  168.8 471.0 %reduce-scatter.9.cloned.1.call-start = ((), (), s32[]{:S(2)}) async-start(), calls=%async_computation.15 | async-start | bytes 7864320 | tf_op jit(solution)/shard_map/reduce_scatter | solution.py:255
  218.3 90.9 %copy-start.39 = (f32[4,768]{1,0:T(4,128)S(1)}, f32[4,768]{1,0:T(4,128)}, u32[]{:S(2)}) copy-start(f32[4,768]{1,0:T(4,128)} %get-tuple-element.256) | copy-start | bytes 36868
  239.4 13.0 %copy-start.19 = (bf16[2,2,256,12,64]{2,4,3,1,0:T(8,128)(2,1)S(1)}, bf16[2,2,256,12,64]{2,4,3,1,0:T(8,128)(2,1)}, u32[]{:S(2)}) copy-start(bf16[2,2,256,12,64]{2,4,3,1,0:T(8,128)(2,1)} %get-tuple-element.417) | copy-start | bytes 4718596 | tf_op jit(solution)/shard_map/while
  314.7 50.6 %copy-start.17 = (f32[4,256,768]{2,1,0:T(8,128)}, f32[4,256,768]{2,1,0:T(8,128)S(1)}, u32[]{:S(2)}) copy-start(f32[4,256,768]{2,1,0:T(8,128)S(1)} %get-tuple-element.222) | copy-start | bytes 9437188
  314.7 50.5 %copy-start.47 = (f32[4,256]{1,0:T(4,128)}, f32[4,256]{1,0:T(4,128)S(1)}, u32[]{:S(2)}) copy-start(f32[4,256]{1,0:T(4,128)S(1)} %broadcast_multiply_fusion.8) | copy-start | bytes 12292
  315.2 50.0 %copy-start.68 = (f32[4,256]{1,0:T(4,128)}, f32[4,256]{1,0:T(4,128)S(1)}, u32[]{:S(2)}) copy-start(f32[4,256]{1,0:T(4,128)S(1)} %add_rsqrt_fusion) | copy-start | bytes 12292
  326.3 28.7 %copy-start.75 = (bf16[768,3072]{1,0:T(8,128)(2,1)S(1)}, bf16[768,3072]{1,0:T(8,128)(2,1)}, u32[]{:S(2)}) copy-start(bf16[768,3072]{1,0:T(8,128)(2,1)} %all-gather.18.cloned.1.call-done) | copy-start | bytes 14155780
  365.3 15.4 %copy-start.32 = (bf16[768,768]{1,0:T(8,128)(2,1)S(1)}, bf16[768,768]{1,0:T(8,128)(2,1)}, u32[]{:S(2)}) copy-start(bf16[768,768]{1,0:T(8,128)(2,1)} %all-gather.16.cloned.1.call-done) | copy-start | bytes 3538948
  435.1 21.7 %copy-start.14 = (f32[2,2,256,12,64]{2,4,3,1,0:T(8,128)S(1)}, f32[2,2,256,12,64]{2,4,3,1,0:T(8,128)}, u32[]{:S(2)}) copy-start(f32[2,2,256,12,64]{2,4,3,1,0:T(8,128)} %get-tuple-element.438) | copy-start | bytes 9437188 | tf_op jit(solution)/shard_map/while
  528.0 21.7 %copy-start.14 = (f32[2,2,256,12,64]{2,4,3,1,0:T(8,128)S(1)}, f32[2,2,256,12,64]{2,4,3,1,0:T(8,128)}, u32[]{:S(2)}) copy-start(f32[2,2,256,12,64]{2,4,3,1,0:T(8,128)} %get-tuple-element.438) | copy-start | bytes 9437188 | tf_op jit(solution)/shard_map/while
  578.6 122.3 %reduce-scatter.11.cloned.1.call-start = ((), (), s32[]{:S(2)}) async-start(), calls=%async_computation.16 | async-start | bytes 7864320 | tf_op jit(solution)/shard_map/reduce_scatter | solution.py:261
  587.4 142.2 %reduce-scatter.15.cloned.1.call-start = ((), (), s32[]{:S(2)}) async-start(), calls=%async_computation.18 | async-start | bytes 1474560 | tf_op jit(solution)/shard_map/reduce_scatter | solution.py:312
  593.9 186.2 %reduce-scatter.19.cloned.1.call-start = ((), (), s32[]{:S(2)}) async-start(), calls=%async_computation.20 | async-start | bytes 5898240 | tf_op jit(solution)/shard_map/reduce_scatter | solution.py:321
  606.7 223.7 %reduce-scatter.17.cloned.1.call-start = ((), (), s32[]{:S(2)}) async-start(), calls=%async_computation.19 | async-start | bytes 5898240 | tf_op jit(solution)/shard_map/reduce_scatter | solution.py:315
  618.6 235.1 %reduce-scatter.23.cloned.1.call-start = ((), (), s32[]{:S(2)}) async-start(), calls=%async_computation.22 | async-start | bytes 327680 | tf_op jit(solution)/shard_map/reduce_scatter | solution.py:339
  623.1 19.9 %copy-start.26 = (f32[4,256,64]{1,2,0:T(8,128)S(1)}, f32[4,256,64]{1,2,0:T(8,128)}, u32[]{:S(2)}) copy-start(f32[4,256,64]{1,2,0:T(8,128)} %copy-done.25) | copy-start | bytes 786436
  659.2 41.6 %copy-start.36 = (f32[4,768]{1,0:T(4,128)S(1)}, f32[4,768]{1,0:T(4,128)}, u32[]{:S(2)}) copy-start(f32[4,768]{1,0:T(4,128)} %copy-done.35) | copy-start | bytes 36868
  659.2 41.6 %copy-start.42 = (f32[4,256]{1,0:T(4,128)S(1)}, f32[4,256]{1,0:T(4,128)}, u32[]{:S(2)}) copy-start(f32[4,256]{1,0:T(4,128)} %copy-done.41) | copy-start | bytes 12292
  659.2 41.6 %copy-start.44 = (f32[768]{0:T(1024)S(1)}, f32[768]{0:T(1024)}, u32[]{:S(2)}) copy-start(f32[768]{0:T(1024)} %copy-done.43) | copy-start | bytes 9220
  659.3 41.6 %copy-start.46 = (f32[4,256]{1,0:T(4,128)S(1)}, f32[4,256]{1,0:T(4,128)}, u32[]{:S(2)}) copy-start(f32[4,256]{1,0:T(4,128)} %copy-done.45) | copy-start | bytes 12292
  712.2 170.2 %reduce-scatter.21.cloned.1.call-start = ((), (), s32[]{:S(2)}) async-start(), calls=%async_computation.21 | async-start | bytes 1474560 | tf_op jit(solution)/shard_map/reduce_scatter | solution.py:327
  717.2 208.3 %reduce-scatter.13.cloned.1.call-start = ((), (), s32[]{:S(2)}) async-start(), calls=%async_computation.17 | async-start | bytes 4423680 | tf_op jit(solution)/shard_map/reduce_scatter | solution.py:309
  725.4 105.1 %copy-start.63 = (bf16[3072]{0:T(1024)(128)(2,1)S(1)}, bf16[3072]{0:T(1024)(128)(2,1)}, u32[]{:S(2)}) copy-start(bf16[3072]{0:T(1024)(128)(2,1)} %get-tuple-element.262) | copy-start | bytes 18436
  725.4 105.1 %copy-start.71 = (bf16[768]{0:T(1024)(128)(2,1)S(1)}, bf16[768]{0:T(1024)(128)(2,1)}, u32[]{:S(2)}) copy-start(bf16[768]{0:T(1024)(128)(2,1)} %get-tuple-element.160) | copy-start | bytes 4612
  841.2 84.3 %copy-start.31 = (bf16[768,768]{1,0:T(8,128)(2,1)S(1)}, bf16[768,768]{1,0:T(8,128)(2,1)}, u32[]{:S(2)}) copy-start(bf16[768,768]{1,0:T(8,128)(2,1)} %reduce-scatter.19.cloned.1.call-done) | copy-start | bytes 3538948
  841.2 84.3 %copy-start.34 = (bf16[192,768]{1,0:T(8,128)(2,1)S(1)}, bf16[192,768]{1,0:T(8,128)(2,1)}, u32[]{:S(2)}) copy-start(bf16[192,768]{1,0:T(8,128)(2,1)} %reduce-scatter.15.cloned.1.call-done) | copy-start | bytes 884740
  841.2 390.7 %copy-start.1 = (bf16[1024,128]{1,0:T(8,128)(2,1)S(1)}, bf16[1024,128]{1,0:T(8,128)(2,1)}, u32[]{:S(2)}) copy-start(bf16[1024,128]{1,0:T(8,128)(2,1)} %param.20) | copy-start | bytes 786436
  (56 other events, 338.3 us)
Sparse Core Ops, SparseCore 0:
  9.6 20.2 all-gather.9
  31.5 30.7 all-gather.11
  73.6 51.7 all-gather.13
  126.9 20.2 all-gather.15
  148.6 47.6 all-gather.17
  197.7 37.4 all-gather.19
  237.3 46.3 all-gather.21
  578.7 60.9 reduce-scatter.8
  642.5 58.3 reduce-scatter.10
  703.9 25.7 reduce-scatter.14
  732.3 47.8 reduce-scatter.18
  782.6 47.8 reduce-scatter.16
  833.6 20.0 reduce-scatter.22
  856.7 25.7 reduce-scatter.20
  885.1 40.4 reduce-scatter.12
